TPU v7x, 32 devices: a whole 2x2x4 slice. The times are simulated.
32 devices in a mesh: row: 4 (over z), col: 8 (over y, x, core).
Axes of the slice: x: 2, y: 2, z: 4, core: 2. Of those that a mesh axis runs over, the one named last changes fastest.
Arguments:
- rhs_front: float32 [4, 6144, 1024], P(None, 'row', 'col'), may hold values from -6 to 6
- lower_blocks: float32 [6, 6144, 6144], P(None, 'row', 'col'), may hold values from -0.046875 to 0.046875
- panel_inverse: float32 [4, 6144, 6144], P(None, 'col', 'row'), may hold values from -0.078125 to 0.078125
- child_rows: float32 [4, 64, 128, 1024], P('row', 'col'), may hold values from -4 to 4
- child_map: int32 [4, 64], P('row', 'col'), may hold values from 0 to 47
- child_owner: int32 [8, 24, 1], P('col'), may hold values from 0 to 3; in each aligned block of 24 rows (0 to 23, 24 to 47, ..., all dimensions but the last counted through in order) at most 7 rows name the same one
Outputs:
- solution: float32 [4, 6144, 1024], P(None, 'col')
- child_rhs: float32 [8, 4, 7, 128, 1024], P('col', 'row')
Inputs may be any that keep to these rules, and one draw needn't show every extreme that they name: `child_map`: several child update blocks may name the same front block. `child_owner`: of the 24 solved blocks of one column group, at most 7 name the same row group, and in some column group one row group is named exactly 7 times.
All inputs are finite; a program needn't handle non-finite values.
Results may differ from a plain program's by a relative error of at most 0.00012.
Values sent between devices are 32-bit elements; how exact they have to be, the bound alone decides.
A program may use at most 192 MiB of HBM per device.

v0:
```python
import jax
import jax.numpy as jnp
from jax import lax
from jax.sharding import PartitionSpec as P


def on_device(rhs_front, lower_blocks, panel_inverse, child_rows, child_map, child_owner):
    highest = lax.Precision.HIGHEST
    row_count = lax.axis_size("row")
    row_at = lax.axis_index("row")
    col_at = lax.axis_index("col")
    panels, row_span, narrow = rhs_front.shape
    col_span = panel_inverse.shape[1]
    block = child_rows.shape[2]
    width = child_rows.shape[3]
    local_blocks = panels * row_span // block
    per_panel = col_span // block
    held_blocks = panels * per_panel
    most = max(2, held_blocks // row_count + 1)
    share = width // row_count
    targets = jnp.arange(local_blocks, dtype=jnp.int32)
    picks = (child_map[0][None, :] == targets[:, None]).astype(jnp.float32)
    added = jnp.einsum("lk,kbr->lbr", picks, child_rows[0], precision=highest).reshape(
        panels, row_span, width
    )
    placed = lax.dynamic_update_slice(
        jnp.zeros((panels, row_span, width), jnp.float32), rhs_front, (0, 0, col_at * narrow)
    )
    assembled = added + placed
    owner = child_owner[0, :, 0]
    hits = (owner[None, :] == jnp.arange(row_count, dtype=jnp.int32)[:, None]).astype(jnp.int32)
    ranks = jnp.cumsum(hits, axis=1) - hits
    slot_match = (ranks[:, None, :] == jnp.arange(most, dtype=jnp.int32)[None, :, None]).astype(
        jnp.int32
    )
    routing = (hits[:, None, :] * slot_match).astype(jnp.float32)
    solved = []
    for panel in range(panels):
        front = assembled[panel]
        for prior in range(panel):
            front = front - jnp.dot(
                lower_blocks[panel * (panel - 1) // 2 + prior],
                solved[prior],
                precision=highest,
                preferred_element_type=jnp.float32,
            )
        front = lax.psum(front, "col")
        partial_value = jnp.dot(
            panel_inverse[panel], front, precision=highest, preferred_element_type=jnp.float32
        )
        current = lax.psum(partial_value, "row")
        solved.append(current)
    solution = jnp.stack(solved)
    mine = lax.dynamic_slice_in_dim(
        solution.reshape(held_blocks, block, width), row_at * share, share, 2
    )
    sending = jnp.einsum("dsk,kbr->dsbr", routing, mine, precision=highest)
    received = lax.all_to_all(sending, "row", split_axis=0, concat_axis=3, tiled=True)
    return (solution, received.reshape(1, 1, most, block, width))


def solution(mesh):
    return jax.shard_map(
        on_device,
        mesh=mesh,
        in_specs=(
            P(None, "row", "col"),
            P(None, "row", "col"),
            P(None, "col", "row"),
            P("row", "col", None, None),
            P("row", "col"),
            P("col", None, None),
        ),
        out_specs=(P(None, "col", None), P("col", "row", None, None, None)),
        check_vma=False,
    )
```

profile of v0, /device:TPU:0, one launch (start us, length us, event | category | flops | bytes accessed | tf_op | source)
XLA Modules:
  0.0 1298.2 jit_solution(18290730721862400627)
XLA Ops:
  7.2 0.0 all-reduce.9.cloned.1.call-start
  7.2 16.1 %fusion.38 = f32[48,128,1024]{2,0,1:T(8,128)S(1)} fusion(f32[8,128,1024]{2,1,0:T(8,128)} %bitcast.124, s32[8]{0:T(128)} %bitcast.129), kind=kOutput, calls=%fused_computation.41 | convolution fusion | flops 603980160 | bytes 29360160 | tf_op jit(solution)/shard_map/lk,kbr->lbr/dot_general | solution.py:23
  23.3 27.6 %copy.18 = f32[48,128,1024]{2,1,0:T(8,128)} copy(f32[48,128,1024]{2,0,1:T(8,128)S(1)} %fusion.38) | data formatting | bytes 50331648 | tf_op jit(solution)/shard_map/lk,kbr->lbr/dot_general | solution.py:23
  50.9 25.1 %copy.21 = f32[4,1536,1024]{1,2,0:T(8,128)} copy(f32[4,1536,1024]{2,1,0:T(8,128)} %bitcast.120) | data formatting | bytes 50331648 | tf_op jit(solution)/shard_map/reshape | solution.py:23
  76.0 2.4 copy.20
  78.4 4.1 add_dynamic-update-slice_fusion
  82.5 5.9 slice_bitcast_fusion.3
  88.4 0.0 all-reduce.9.cloned.1.call-update
  88.4 0.0 all-reduce.11.cloned.1.call-start
  88.5 106.8 %all-reduce.9.cloned.1.call-done = f32[1536,1024]{0,1:T(8,128)} async-done(((f32[1536,1024]{0,1:T(8,128)}), f32[1536,1024]{0,1:T(8,128)}) %all-reduce.9.cloned.1.call-update) | async-done | bytes 6291472 | tf_op jit(solution)/shard_map/psum | solution.py:47
  195.3 19.5 %fusion.45 = f32[768,1024]{0,1:T(8,128)} fusion(f32[1536,1024]{0,1:T(8,128)} %all-reduce.9.cloned.1.call-done, f32[4,768,1536]{2,1,0:T(8,128)} %param.8), kind=kOutput, calls=%fused_computation.46 | convolution fusion | flops 14495514624 | bytes 14155776 | tf_op jit(solution)/shard_map/dot_general | solution.py:48
  214.8 0.0 all-reduce.11.cloned.1.call-update
  214.8 0.0 all-reduce.13.cloned.1.call-start
  214.9 121.3 %all-reduce.11.cloned.1.call-done = f32[768,1024]{0,1:T(8,128)} async-done(((f32[768,1024]{0,1:T(8,128)}), f32[768,1024]{0,1:T(8,128)}) %all-reduce.11.cloned.1.call-update) | async-done | bytes 3145744 | tf_op jit(solution)/shard_map/psum | solution.py:51
  336.1 19.6 %fusion.5 = f32[1536,1024]{0,1:T(8,128)} fusion(f32[4,1536,1024]{1,2,0:T(8,128)} %add_dynamic-update-slice_fusion, f32[768,1024]{0,1:T(8,128)} %all-reduce.11.cloned.1.call-done, f32[6,1536,768]{2,1,0:T(8,128)} %param.7), kind=kOutput, calls=%fused_computation.9 | convolution fusion | flops 14497087488 | bytes 20447232 | tf_op jit(solution)/shard_map/dot_general | solution.py:41
  355.8 0.0 all-reduce.13.cloned.1.call-update
  355.8 0.0 all-reduce.15.cloned.1.call-start
  355.8 103.0 %all-reduce.13.cloned.1.call-done = f32[1536,1024]{0,1:T(8,128)} async-done(((f32[1536,1024]{0,1:T(8,128)}), f32[1536,1024]{0,1:T(8,128)}) %all-reduce.13.cloned.1.call-update) | async-done | bytes 6291472 | tf_op jit(solution)/shard_map/psum | solution.py:47
  458.9 19.6 %fusion.48 = f32[768,1024]{0,1:T(8,128)} fusion(f32[1536,1024]{0,1:T(8,128)} %all-reduce.13.cloned.1.call-done, f32[4,768,1536]{2,1,0:T(8,128)} %param.8), kind=kOutput, calls=%fused_computation.47 | convolution fusion | flops 14495514624 | bytes 14155776 | tf_op jit(solution)/shard_map/dot_general | solution.py:48
  478.5 0.0 all-reduce.15.cloned.1.call-update
  478.5 0.0 all-reduce.17.cloned.1.call-start
  478.6 121.3 %all-reduce.15.cloned.1.call-done = f32[768,1024]{0,1:T(8,128)} async-done(((f32[768,1024]{0,1:T(8,128)}), f32[768,1024]{0,1:T(8,128)}) %all-reduce.15.cloned.1.call-update) | async-done | bytes 3145744 | tf_op jit(solution)/shard_map/psum | solution.py:51
  599.8 18.3 %fusion.16 = f32[1024,1536]{1,0:T(8,128)S(1)} fusion(f32[768,1024]{0,1:T(8,128)} %all-reduce.15.cloned.1.call-done, f32[6,1536,768]{2,1,0:T(8,128)} %param.7), kind=kOutput, calls=%fused_computation.21 | convolution fusion | flops 14495514624 | bytes 14155776 | tf_op jit(solution)/shard_map/dot_general | solution.py:41
  618.1 19.5 %fusion.4 = f32[1536,1024]{0,1:T(8,128)} fusion(f32[4,1536,1024]{1,2,0:T(8,128)} %add_dynamic-update-slice_fusion, f32[1024,1536]{1,0:T(8,128)S(1)} %fusion.16, f32[768,1024]{0,1:T(8,128)S(1)} %copy-done, f32[6,1536,768]{2,1,0:T(8,128)} %param.7), kind=kOutput, calls=%fused_computation.7 | convolution fusion | flops 14498660352 | bytes 26738688 | tf_op jit(solution)/shard_map/dot_general | solution.py:41
  637.6 0.0 all-reduce.17.cloned.1.call-update
  637.7 0.0 all-reduce.19.cloned.1.call-start
  637.7 103.0 %all-reduce.17.cloned.1.call-done = f32[1536,1024]{0,1:T(8,128)} async-done(((f32[1536,1024]{0,1:T(8,128)}), f32[1536,1024]{0,1:T(8,128)}) %all-reduce.17.cloned.1.call-update) | async-done | bytes 6291472 | tf_op jit(solution)/shard_map/psum | solution.py:47
  740.7 19.5 %fusion.51 = f32[768,1024]{0,1:T(8,128)} fusion(f32[1536,1024]{0,1:T(8,128)} %all-reduce.17.cloned.1.call-done, f32[4,768,1536]{2,1,0:T(8,128)} %param.8), kind=kOutput, calls=%fused_computation.48 | convolution fusion | flops 14495514624 | bytes 14155776 | tf_op jit(solution)/shard_map/dot_general | solution.py:48
  760.2 0.0 all-reduce.19.cloned.1.call-update
  760.3 0.0 all-reduce.21.cloned.1.call-start
  760.3 20.1 %fusion.10 = f32[1024,1536]{1,0:T(8,128)} fusion(f32[768,1024]{0,1:T(8,128)} %all-reduce.15.cloned.1.call-done, f32[6,1536,768]{2,1,0:T(8,128)} %param.7), kind=kOutput, calls=%fused_computation.15 | convolution fusion | flops 14495514624 | bytes 14155776 | tf_op jit(solution)/shard_map/dot_general | solution.py:41
  780.4 101.2 %all-reduce.19.cloned.1.call-done = f32[768,1024]{0,1:T(8,128)} async-done(((f32[768,1024]{0,1:T(8,128)}), f32[768,1024]{0,1:T(8,128)}) %all-reduce.19.cloned.1.call-update) | async-done | bytes 3145744 | tf_op jit(solution)/shard_map/psum | solution.py:51
  881.6 18.8 %fusion.8 = f32[1024,1536]{1,0:T(8,128)S(1)} fusion(f32[768,1024]{0,1:T(8,128)} %all-reduce.19.cloned.1.call-done, f32[6,1536,768]{2,1,0:T(8,128)} %param.7), kind=kOutput, calls=%fused_computation.13 | convolution fusion | flops 14495514624 | bytes 14155776 | tf_op jit(solution)/shard_map/dot_general | solution.py:41
  900.4 19.7 %fusion.2 = f32[1536,1024]{0,1:T(8,128)} fusion(f32[4,1536,1024]{1,2,0:T(8,128)} %add_dynamic-update-slice_fusion, f32[1024,1536]{1,0:T(8,128)S(1)} %fusion.8, f32[1024,1536]{1,0:T(8,128)S(1)} %copy-done.1, f32[768,1024]{0,1:T(8,128)S(1)} %copy-done, f32[6,1536,768]{2,1,0:T(8,128)} %param.7), kind=kOutput, calls=%fused_computation.4 | convolution fusion | flops 14500233216 | bytes 33030144 | tf_op jit(solution)/shard_map/dot_general | solution.py:41
  920.1 0.0 all-reduce.23.cloned.1.call-start
  920.2 103.0 %all-reduce.21.cloned.1.call-done = f32[1536,1024]{0,1:T(8,128)} async-done(((f32[1536,1024]{0,1:T(8,128)}), f32[1536,1024]{0,1:T(8,128)}) %all-reduce.21.cloned.1.call-update) | async-done | bytes 6291472 | tf_op jit(solution)/shard_map/psum | solution.py:47
  1023.2 19.7 %fusion.54 = f32[1,768,1024]{1,2,0:T(8,128)} fusion(f32[1536,1024]{0,1:T(8,128)} %all-reduce.21.cloned.1.call-done, f32[4,768,1536]{2,1,0:T(8,128)} %param.8), kind=kOutput, calls=%fused_computation.49 | convolution fusion | flops 14495514624 | bytes 14155776 | tf_op jit(solution)/shard_map/dot_general | solution.py:48
  1042.9 0.0 all-reduce.23.cloned.1.call-update
  1042.9 0.2 reduce_window_sum.11
  1043.1 121.1 %all-reduce.23.cloned.1.call-done = f32[1,768,1024]{1,2,0:T(8,128)} async-done(((f32[1,768,1024]{1,2,0:T(8,128)}), f32[1,768,1024]{1,2,0:T(8,128)}) %all-reduce.23.cloned.1.call-update) | async-done | bytes 3145744 | tf_op jit(solution)/shard_map/psum | solution.py:51
  1164.2 9.1 pad_maximum_fusion
  1173.3 12.6 copy.26
  1185.9 2.2 constant_dynamic-slice_fusion
  1188.1 6.7 fusion.44
  1194.8 1.1 copy.24
  1196.0 85.4 %all_to_all.15 = f32[4,7,128,256]{3,2,1,0:T(8,128)} all-to-all(f32[4,7,128,256]{3,2,1,0:T(8,128)S(1)} %copy.24), channel_id=1, replica_groups=mesh['row'=4,'col'=8] {'row'}, dimensions={0} | all-to-all | bytes 7340032 | tf_op jit(solution)/shard_map/all_to_all | solution.py:58
  1281.4 4.6 copy.25
  1286.0 5.0 copy.27
  (9 shorter events, 0.0 us)
Async XLA Ops:
  7.2 188.1 %all-reduce.9.cloned.1.call-start = ((), (), s32[]{:S(2)}) async-start(), calls=%async_computation.1 | async-start | bytes 12582912 | tf_op jit(solution)/shard_map/psum | solution.py:47
  88.4 247.7 %all-reduce.11.cloned.1.call-start = ((), (), s32[]{:S(2)}) async-start(), calls=%async_computation.2 | async-start | bytes 6291456 | tf_op jit(solution)/shard_map/psum | solution.py:51
  214.8 244.0 %all-reduce.13.cloned.1.call-start = ((), (), s32[]{:S(2)}) async-start(), calls=%async_computation.3 | async-start | bytes 12582912 | tf_op jit(solution)/shard_map/psum | solution.py:47
  355.8 244.1 %all-reduce.15.cloned.1.call-start = ((), (), s32[]{:S(2)}) async-start(), calls=%async_computation.4 | async-start | bytes 6291456 | tf_op jit(solution)/shard_map/psum | solution.py:51
  478.5 139.6 %copy-start = (f32[768,1024]{0,1:T(8,128)S(1)}, f32[768,1024]{0,1:T(8,128)}, u32[]{:S(2)}) copy-start(f32[768,1024]{0,1:T(8,128)} %all-reduce.11.cloned.1.call-done) | copy-start | bytes 9437188
  478.5 262.2 %all-reduce.17.cloned.1.call-start = ((), (), s32[]{:S(2)}) async-start(), calls=%async_computation.5 | async-start | bytes 12582912 | tf_op jit(solution)/shard_map/psum | solution.py:47
  637.7 243.9 %all-reduce.19.cloned.1.call-start = ((), (), s32[]{:S(2)}) async-start(), calls=%async_computation.6 | async-start | bytes 6291456 | tf_op jit(solution)/shard_map/psum | solution.py:51
  760.3 262.9 %all-reduce.21.cloned.1.call-start = ((), (), s32[]{:S(2)}) async-start(), calls=%async_computation.7 | async-start | bytes 12582912 | tf_op jit(solution)/shard_map/psum | solution.py:47
  881.6 18.8 %copy-start.1 = (f32[1024,1536]{1,0:T(8,128)S(1)}, f32[1024,1536]{1,0:T(8,128)}, u32[]{:S(2)}) copy-start(f32[1024,1536]{1,0:T(8,128)} %fusion.10) | copy-start | bytes 18874372
  920.1 122.8 %copy-start.2 = (s32[1,24,1]{1,2,0:T(1,128)S(1)}, s32[1,24,1]{1,2,0:T(1,128)}, u32[]{:S(2)}) copy-start(s32[1,24,1]{1,2,0:T(1,128)} %param.11) | copy-start | bytes 292
  920.1 244.1 %all-reduce.23.cloned.1.call-start = ((), (), s32[]{:S(2)}) async-start(), calls=%async_computation.8 | async-start | bytes 6291456 | tf_op jit(solution)/shard_map/psum | solution.py:51
Sparse Core Ops, SparseCore 0:
  88.6 106.6 all-reduce.8
  214.9 121.1 all-reduce.10
  355.9 102.9 all-reduce.12
  478.6 121.1 all-reduce.14
  637.8 102.9 all-reduce.16
  760.4 121.1 all-reduce.18
  920.2 102.8 all-reduce.20
  1043.0 121.1 all-reduce.22
where the time goes:
time: 1310 us; the launch traced here: 1300 us
  waiting for transfers between devices  881 us (67%)
  matrix products  217 us (17%)
  local copies, waits for them, and re-layouts  86.5 us (7%)
  blocking collectives  85.4 us (7%)
  between operations  14.6 us (1%)
  other arithmetic  13.4 us (1%)
    psum x4, waiting for transfers between devices, on_device(): current = lax.psum(partial_value, 'row')  465 us
    psum x4, waiting for transfers between devices, on_device(): front = lax.psum(front, 'col')  416 us
    dot_general x6, matrix products, on_device(): jnp.dot(lower_blocks[panel * (panel - 1) // 2 + prior], solved[prior], pr...  116 us
    all_to_all x1, blocking collectives, on_device(): lax.all_to_all(sending, 'row', split_axis=0, concat_axis=3, tiled=True)  85.4 us
    dot_general x4, matrix products, on_device(): jnp.dot(panel_inverse[panel], front, precision=highest, preferred_element...  78.3 us
    dot_general x1, local copies, waits for them, and re-layouts, on_device(): jnp.einsum('lk,kbr->lbr', picks, child_rows[0], precision=highest)  27.6 us
  transfers between devices with their start and end apart: 8, of which 8 were waited for; matrix products, arithmetic and copies ran while one was open for 2% of the time, Pallas kernels for 0%

commit v1 on v0

--- a/solution.py
+++ b/solution.py
@@ -2,6 +2,15 @@
 import jax.numpy as jnp
 from jax import lax
 from jax.sharding import PartitionSpec as P
+
+
+def add_in_pairs(array, axis):
+    size = lax.axis_size(axis)
+    total, far = (array, 1)
+    while far < size:
+        total = total + lax.ppermute(total, axis, [(i, i ^ far) for i in range(size)])
+        far = 2 * far
+    return total
 
 
 def on_device(rhs_front, lower_blocks, panel_inverse, child_rows, child_map, child_owner):
@@ -44,7 +53,7 @@
                 precision=highest,
                 preferred_element_type=jnp.float32,
             )
-        front = lax.psum(front, "col")
+        front = add_in_pairs(front, "col")
         partial_value = jnp.dot(
             panel_inverse[panel], front, precision=highest, preferred_element_type=jnp.float32
         )

time: 1310 us -> 2050 us (1.56)
  waiting for transfers between devices: 881 us -> 1590 us
  other arithmetic: 13.4 us -> 38.4 us
    ppermute x0 -> x12, waiting for transfers between devices: none -> 1130 us  [add_in_pairs(): lax.ppermute(total, axis, [(i, i ^ far) for i in range(size)])]
    psum x4 -> x0, waiting for transfers between devices: 416 us -> none  [on_device(): front = lax.psum(front, 'col')]
    add x0 -> x8, other arithmetic: none -> 25 us  [add_in_pairs(): total + lax.ppermute(total, axis, [(i, i ^ far) for i in range(size)])]
  transfers between devices with their start and end apart: 8 -> 16, of which waited for: 8 -> 16; matrix products, arithmetic and copies ran while one was open for 2% -> 1% of each run, Pallas kernels for 0% -> 0%
where the time goes in v1:
time: 2050 us; the launch traced here: 2040 us
  waiting for transfers between devices  1590 us (78%)
  matrix products  210 us (10%)
  blocking collectives  85.4 us (4%)
  local copies, waits for them, and re-layouts  83.7 us (4%)
  other arithmetic  38.4 us (2%)
    ppermute x12, waiting for transfers between devices, add_in_pairs(): lax.ppermute(total, axis, [(i, i ^ far) for i in range(size)])  1130 us
    psum x4, waiting for transfers between devices, on_device(): current = lax.psum(partial_value, 'row')  463 us
    dot_general x6, matrix products, on_device(): jnp.dot(lower_blocks[panel * (panel - 1) // 2 + prior], solved[prior], pr...  115 us
    all_to_all x1, blocking collectives, on_device(): lax.all_to_all(sending, 'row', split_axis=0, concat_axis=3, tiled=True)  85.4 us
    dot_general x4, matrix products, on_device(): jnp.dot(panel_inverse[panel], front, precision=highest, preferred_element...  72.6 us
  transfers between devices with their start and end apart: 16, of which 16 were waited for; matrix products, arithmetic and copies ran while one was open for 1% of the time, Pallas kernels for 0%

profile of v1, /device:TPU:0, one launch (start us, length us, event | category | flops | bytes accessed | tf_op | source)
XLA Modules:
  0.0 2036.0 jit_solution(3340305420311828483)
XLA Ops:
  7.2 16.1 fusion.42
  23.3 27.5 %copy.22 = f32[48,128,1024]{2,1,0:T(8,128)} copy(f32[48,128,1024]{2,0,1:T(8,128)S(1)} %fusion.42) | data formatting | bytes 50331648 | tf_op jit(solution)/shard_map/lk,kbr->lbr/dot_general | solution.py:32
  50.8 24.9 %copy.25 = f32[4,1536,1024]{1,2,0:T(8,128)} copy(f32[4,1536,1024]{2,1,0:T(8,128)} %bitcast.118) | data formatting | bytes 50331648 | tf_op jit(solution)/shard_map/reshape | solution.py:32
  75.7 2.4 copy.24
  78.1 4.1 add_dynamic-update-slice_fusion
  82.2 3.2 slice_bitcast_fusion.3
  86.0 9.8 collective-permute-done
  95.8 4.2 fusion.81
  99.9 2.9 collective-permute-start.1
  102.9 135.8 %collective-permute-done.1 = f32[1536,1024]{0,1:T(8,128)S(1)} collective-permute-done((f32[1536,1024]{0,1:T(8,128)S(1)}, f32[1536,1024]{0,1:T(8,128)S(1)}, u32[]{:S(2)}, u32[]{:S(2)}) %collective-permute-start.1) | collective-permute-done | bytes 6291488 | tf_op jit(solution)/shard_map/ppermute | solution.py:11
  240.1 1.9 collective-permute-start.2
  241.9 135.2 %collective-permute-done.2 = f32[1536,1024]{0,1:T(8,128)S(1)} collective-permute-done((f32[1536,1024]{0,1:T(8,128)S(1)}, f32[1536,1024]{0,1:T(8,128)S(1)}, u32[]{:S(2)}, u32[]{:S(2)}) %collective-permute-start.2) | collective-permute-done | bytes 6291488 | tf_op jit(solution)/shard_map/ppermute | solution.py:11
  377.1 18.0 fusion.49
  395.2 122.4 %all-reduce.5.cloned.1.call-done = f32[768,1024]{0,1:T(8,128)} async-done(((f32[768,1024]{0,1:T(8,128)}), f32[768,1024]{0,1:T(8,128)}) %all-reduce.5.cloned.1.call-update) | async-done | bytes 3145744 | tf_op jit(solution)/shard_map/psum | solution.py:60
  517.6 19.5 fusion.5
  537.2 10.1 collective-permute-done.3
  550.3 136.1 %collective-permute-done.4 = f32[1536,1024]{0,1:T(8,128)S(1)} collective-permute-done((f32[1536,1024]{0,1:T(8,128)S(1)}, f32[1536,1024]{0,1:T(8,128)S(1)}, u32[]{:S(2)}, u32[]{:S(2)}) %collective-permute-start.4) | collective-permute-done | bytes 6291488 | tf_op jit(solution)/shard_map/ppermute | solution.py:11
  687.8 1.5 collective-permute-start.5
  689.3 135.2 %collective-permute-done.5 = f32[1536,1024]{0,1:T(8,128)S(1)} collective-permute-done((f32[1536,1024]{0,1:T(8,128)S(1)}, f32[1536,1024]{0,1:T(8,128)S(1)}, u32[]{:S(2)}, u32[]{:S(2)}) %collective-permute-start.5) | collective-permute-done | bytes 6291488 | tf_op jit(solution)/shard_map/ppermute | solution.py:11
  824.5 18.4 fusion.54
  843.0 120.2 %all-reduce.7.cloned.1.call-done = f32[768,1024]{0,1:T(8,128)} async-done(((f32[768,1024]{0,1:T(8,128)}), f32[768,1024]{0,1:T(8,128)}) %all-reduce.7.cloned.1.call-update) | async-done | bytes 3145744 | tf_op jit(solution)/shard_map/psum | solution.py:60
  963.2 18.3 fusion.22
  981.4 18.8 fusion.4
  1000.3 10.3 collective-permute-done.6
  1010.6 4.2 add.62
  1016.3 136.2 %collective-permute-done.7 = f32[1536,1024]{0,1:T(8,128)} collective-permute-done((f32[1536,1024]{0,1:T(8,128)S(1)}, f32[1536,1024]{0,1:T(8,128)}, u32[]{:S(2)}, u32[]{:S(2)}) %collective-permute-start.7) | collective-permute-done | bytes 6291488 | tf_op jit(solution)/shard_map/ppermute | solution.py:11
  1152.5 4.2 add.63
  1158.2 135.2 %collective-permute-done.8 = f32[1536,1024]{0,1:T(8,128)S(1)} collective-permute-done((f32[1536,1024]{0,1:T(8,128)S(1)}, f32[1536,1024]{0,1:T(8,128)S(1)}, u32[]{:S(2)}, u32[]{:S(2)}) %collective-permute-start.8) | collective-permute-done | bytes 6291488 | tf_op jit(solution)/shard_map/ppermute | solution.py:11
  1293.4 18.0 fusion.59
  1311.5 19.7 fusion.17
  1331.2 100.5 %all-reduce.9.cloned.1.call-done = f32[768,1024]{0,1:T(8,128)} async-done(((f32[768,1024]{0,1:T(8,128)}), f32[768,1024]{0,1:T(8,128)}) %all-reduce.9.cloned.1.call-update) | async-done | bytes 3145744 | tf_op jit(solution)/shard_map/psum | solution.py:60
  1431.7 19.1 fusion.15
  1450.8 19.6 fusion.2
  1470.5 10.3 collective-permute-done.9
  1480.8 4.2 add.65
  1486.5 136.2 %collective-permute-done.10 = f32[1536,1024]{0,1:T(8,128)} collective-permute-done((f32[1536,1024]{0,1:T(8,128)S(1)}, f32[1536,1024]{0,1:T(8,128)}, u32[]{:S(2)}, u32[]{:S(2)}) %collective-permute-start.10) | collective-permute-done | bytes 6291488 | tf_op jit(solution)/shard_map/ppermute | solution.py:11
  1622.6 4.2 add.66
  1626.8 1.5 collective-permute-start.11
  1628.4 135.2 %collective-permute-done.11 = f32[1536,1024]{0,1:T(8,128)S(1)} collective-permute-done((f32[1536,1024]{0,1:T(8,128)S(1)}, f32[1536,1024]{0,1:T(8,128)S(1)}, u32[]{:S(2)}, u32[]{:S(2)}) %collective-permute-start.11) | collective-permute-done | bytes 6291488 | tf_op jit(solution)/shard_map/ppermute | solution.py:11
  1763.6 18.2 fusion.64
  1782.1 120.0 %all-reduce.11.cloned.1.call-done = f32[1,768,1024]{1,2,0:T(8,128)} async-done(((f32[1,768,1024]{1,2,0:T(8,128)}), f32[1,768,1024]{1,2,0:T(8,128)}) %all-reduce.11.cloned.1.call-update) | async-done | bytes 3145744 | tf_op jit(solution)/shard_map/psum | solution.py:60
  1902.0 9.1 pad_maximum_fusion
  1911.1 12.8 copy.30
  1924.0 2.2 constant_dynamic-slice_fusion
  1926.2 6.7 fusion.48
  1934.1 85.4 %all_to_all.15 = f32[4,7,128,256]{3,2,1,0:T(8,128)} all-to-all(f32[4,7,128,256]{3,2,1,0:T(8,128)S(1)} %copy.28), channel_id=1, replica_groups=mesh['row'=4,'col'=8] {'row'}, dimensions={0} | all-to-all | bytes 7340032 | tf_op jit(solution)/shard_map/all_to_all | solution.py:67
  2019.4 4.6 copy.29
  2024.0 5.0 copy.31
  (29 shorter events, 12.6 us)
Async XLA Ops:
  7.2 510.4 %all-reduce.5.cloned.1.call-start = ((), (), s32[]{:S(2)}) async-start(), calls=%async_computation.1 | async-start | bytes 6291456 | tf_op jit(solution)/shard_map/psum | solution.py:60
  85.4 10.3 collective-permute-start
  99.9 138.7 %collective-permute-start.1 = (f32[1536,1024]{0,1:T(8,128)S(1)}, f32[1536,1024]{0,1:T(8,128)S(1)}, u32[]{:S(2)}, u32[]{:S(2)}) collective-permute-start(f32[1536,1024]{0,1:T(8,128)S(1)} %fusion.81), channel_id=1, source_target_pairs={{0,2},{1,3},{2,0},{3,1},{4,6},{5,7},{6,4},{7,5},{8,10},{9,11},{10,... | collective-permute-start | bytes 18874376 | tf_op jit(solution)/shard_map/ppermute | solution.py:11
  240.1 137.0 %collective-permute-start.2 = (f32[1536,1024]{0,1:T(8,128)S(1)}, f32[1536,1024]{0,1:T(8,128)S(1)}, u32[]{:S(2)}, u32[]{:S(2)}) collective-permute-start(f32[1536,1024]{0,1:T(8,128)S(1)} %add.57), channel_id=1, source_target_pairs={{0,4},{1,5},{2,6},{3,7},{4,0},{5,1},{6,2},{7,3},{8,12},{9,13},{10,... | collective-permute-start | bytes 18874376 | tf_op jit(solution)/shard_map/ppermute | solution.py:11
  395.2 568.0 %all-reduce.7.cloned.1.call-start = ((), (), s32[]{:S(2)}) async-start(), calls=%async_computation.2 | async-start | bytes 6291456 | tf_op jit(solution)/shard_map/psum | solution.py:60
  537.1 10.2 collective-permute-start.3
  548.7 137.6 %collective-permute-start.4 = (f32[1536,1024]{0,1:T(8,128)S(1)}, f32[1536,1024]{0,1:T(8,128)S(1)}, u32[]{:S(2)}, u32[]{:S(2)}) collective-permute-start(f32[1536,1024]{0,1:T(8,128)S(1)} %add.59), channel_id=1, source_target_pairs={{0,2},{1,3},{2,0},{3,1},{4,6},{5,7},{6,4},{7,5},{8,10},{9,11},{10,... | collective-permute-start | bytes 18874376 | tf_op jit(solution)/shard_map/ppermute | solution.py:11
  687.8 136.8 %collective-permute-start.5 = (f32[1536,1024]{0,1:T(8,128)S(1)}, f32[1536,1024]{0,1:T(8,128)S(1)}, u32[]{:S(2)}, u32[]{:S(2)}) collective-permute-start(f32[1536,1024]{0,1:T(8,128)S(1)} %add.60), channel_id=1, source_target_pairs={{0,4},{1,5},{2,6},{3,7},{4,0},{5,1},{6,2},{7,3},{8,12},{9,13},{10,... | collective-permute-start | bytes 18874376 | tf_op jit(solution)/shard_map/ppermute | solution.py:11
  843.0 138.5 %copy-start = (f32[768,1024]{0,1:T(8,128)S(1)}, f32[768,1024]{0,1:T(8,128)}, u32[]{:S(2)}) copy-start(f32[768,1024]{0,1:T(8,128)} %all-reduce.5.cloned.1.call-done) | copy-start | bytes 9437188
  843.0 588.7 %all-reduce.9.cloned.1.call-start = ((), (), s32[]{:S(2)}) async-start(), calls=%async_computation.3 | async-start | bytes 6291456 | tf_op jit(solution)/shard_map/psum | solution.py:60
  1000.2 10.4 collective-permute-start.6
  1014.8 137.7 %collective-permute-start.7 = (f32[1536,1024]{0,1:T(8,128)S(1)}, f32[1536,1024]{0,1:T(8,128)}, u32[]{:S(2)}, u32[]{:S(2)}) collective-permute-start(f32[1536,1024]{0,1:T(8,128)S(1)} %add.62), channel_id=1, source_target_pairs={{0,2},{1,3},{2,0},{3,1},{4,6},{5,7},{6,4},{7,5},{8,10},{9,11},{10,... | collective-permute-start | bytes 18874376 | tf_op jit(solution)/shard_map/ppermute | solution.py:11
  1156.7 136.8 %collective-permute-start.8 = (f32[1536,1024]{0,1:T(8,128)S(1)}, f32[1536,1024]{0,1:T(8,128)S(1)}, u32[]{:S(2)}, u32[]{:S(2)}) collective-permute-start(f32[1536,1024]{0,1:T(8,128)S(1)} %add.63), channel_id=1, source_target_pairs={{0,4},{1,5},{2,6},{3,7},{4,0},{5,1},{6,2},{7,3},{8,12},{9,13},{10,... | collective-permute-start | bytes 18874376 | tf_op jit(solution)/shard_map/ppermute | solution.py:11
  1311.5 590.6 %all-reduce.11.cloned.1.call-start = ((), (), s32[]{:S(2)}) async-start(), calls=%async_computation.4 | async-start | bytes 6291456 | tf_op jit(solution)/shard_map/psum | solution.py:60
  1431.7 19.1 copy-start.1
  1470.4 10.4 collective-permute-start.9
  1484.9 137.7 %collective-permute-start.10 = (f32[1536,1024]{0,1:T(8,128)S(1)}, f32[1536,1024]{0,1:T(8,128)}, u32[]{:S(2)}, u32[]{:S(2)}) collective-permute-start(f32[1536,1024]{0,1:T(8,128)S(1)} %add.65), channel_id=1, source_target_pairs={{0,2},{1,3},{2,0},{3,1},{4,6},{5,7},{6,4},{7,5},{8,10},{9,11},{10,... | collective-permute-start | bytes 18874376 | tf_op jit(solution)/shard_map/ppermute | solution.py:11
  1626.8 155.0 %copy-start.2 = (s32[1,24,1]{1,2,0:T(1,128)S(1)}, s32[1,24,1]{1,2,0:T(1,128)}, u32[]{:S(2)}) copy-start(s32[1,24,1]{1,2,0:T(1,128)} %param.11) | copy-start | bytes 292
  1626.8 136.8 %collective-permute-start.11 = (f32[1536,1024]{0,1:T(8,128)S(1)}, f32[1536,1024]{0,1:T(8,128)S(1)}, u32[]{:S(2)}, u32[]{:S(2)}) collective-permute-start(f32[1536,1024]{0,1:T(8,128)S(1)} %add.66), channel_id=1, source_target_pairs={{0,4},{1,5},{2,6},{3,7},{4,0},{5,1},{6,2},{7,3},{8,12},{9,13},{10,... | collective-permute-start | bytes 18874376 | tf_op jit(solution)/shard_map/ppermute | solution.py:11
Sparse Core Ops, SparseCore 0:
  395.3 122.2 all-reduce.4
  843.1 120.0 all-reduce.6
  1311.6 120.0 all-reduce.8
  1782.0 120.0 all-reduce.10
